TPU v7x, 128 devices: a whole 4x4x4 slice. The times are simulated.
128 devices in a mesh: blk: 8 (over x_lo, y), grid: 16 (over x_hi, z, core).
Axes of the slice: x: 4 (x_hi: 2, x_lo: 2; x = x_hi * 2 + x_lo), y: 4, z: 4, core: 2. Of those that a mesh axis runs over, the one named last changes fastest.
Arguments:
- conn: int32 [2048, 9], P(('blk', 'grid')), may hold values from 0 to 2047, as said below
- extract: float32 [9, 9, 2048], P(None, None, ('blk', 'grid')), may hold values from 0.1 to 1
- points: float32 [3, 9, 2048], P(None, None, ('blk', 'grid')), as said below
Outputs:
- factor: float32 [1, 2048, 2, 1024], P(None, 'grid', None, 'blk')
Inputs may be any that keep to these rules, and one draw needn't show every extreme that they name: `conn`: element e = ix 32 + iy of the periodic 64 x 32 grid of elements names the functions ((ix + s) mod 64) * 32 + (iy + t) mod 32 for s, t in 0, 1, 2, each once, in an order that differs from element to element. The 9 points of element e = ix 32 + iy are the 3 x 3 Gauss points of the cell [ix / 64, (ix + 1) / 64] x [iy / 64, (iy + 1) / 64], each coordinate then moved by at most 3.5 / 64; points[2] is positive.
All inputs are finite; a program needn't handle non-finite values.
Results may differ from a plain program's by a relative error of at most 0.0003.
Values sent between devices are 32-bit elements; how exact they have to be, the bound alone decides.
A program may use at most 128 MiB of HBM per device.

v0:
```python
import math
import jax
import jax.numpy as jnp
from jax import lax
from jax.sharding import PartitionSpec as P

M = 2048
EX = 64
EY = 32
QP = 9
TB = 128
kernel_gain = 0.02
mass_shift = 0.05


def spread(array, axis, root):
    mine = lax.axis_index(axis) == root
    return lax.psum(jnp.where(mine, array, jnp.zeros_like(array)), axis)


def bernstein_table():
    spread_root = 0.5 * math.sqrt(0.6)
    gauss_nodes = [0.5 - spread_root, 0.5, 0.5 + spread_root]

    def bern_poly(which, where):
        return [(1.0 - where) ** 2, 2.0 * where * (1.0 - where), where * where][which]

    table_rows = []
    for i in range(3):
        for j in range(3):
            table_row = []
            for a in range(3):
                for b in range(3):
                    table_row.append(bern_poly(a, gauss_nodes[i]) * bern_poly(b, gauss_nodes[j]))
            table_rows.append(table_row)
    return jnp.asarray(table_rows, jnp.float32)


def torus_square(first_x, first_y, second_x, second_y):
    height = EY / EX
    gap_x = jnp.abs(first_x - second_x)
    gap_x = jnp.minimum(gap_x, jnp.abs(1.0 - gap_x))
    gap_y = jnp.abs(first_y - second_y)
    gap_y = jnp.minimum(gap_y, jnp.abs(height - gap_y))
    return gap_x * gap_x + gap_y * gap_y


def kernel_rows(test_x, test_y, trial_x, trial_y, trial_w):
    distance = torus_square(test_x[:, None], test_y[:, None], trial_x[None, :], trial_y[None, :])
    return kernel_gain * trial_w[None, :] * (1.0 + distance * (EX * EX / 4.0)) ** (-1.75)


def local_values(extract_cube):
    return jnp.einsum(
        "kb,abn->nka", bernstein_table(), extract_cube, precision=lax.Precision.HIGHEST
    )


def basis_rows(values, links):
    count = links.shape[0]
    slot = jnp.arange(count * QP, dtype=jnp.int32).reshape(count, QP)
    row_index = jnp.broadcast_to(slot[:, :, None], (count, QP, QP))
    col_index = jnp.broadcast_to(links[:, None, :], (count, QP, QP))
    return jnp.zeros((count * QP, M), jnp.float32).at[row_index, col_index].add(values)


def window_width():
    wide = 128 + 4 * EY
    return wide


def fold_window(potential_wide):
    extra = potential_wide.shape[1] - M
    return potential_wide[:, :M] + jnp.pad(potential_wide[:, M:], ((0, 0), (0, M - extra)))


def tile_target(links, grid_size, tile_rows):
    tile = links // TB
    return tile % grid_size * (tile_rows * TB) + tile // grid_size * TB + links % TB


def add_potential(state, piece, first_element, test_x, test_y):
    points_flat, extract_flat, links_flat = piece
    count = points_flat.shape[1]
    span = math.gcd(count, 128)
    width = window_width()
    window_iota = jnp.arange(width, dtype=jnp.int32)

    def step(index, inner):
        potential_wide, total = inner
        first = index * span
        part_points = lax.dynamic_slice_in_dim(points_flat, first, span, 1).reshape(3, QP, span)
        part_extract = lax.dynamic_slice_in_dim(extract_flat, first, span, 1).reshape(QP, QP, span)
        part_links = lax.dynamic_slice_in_dim(links_flat, first, span, 1).T
        kernel_block = kernel_rows(
            test_x,
            test_y,
            part_points[0].T.reshape(-1),
            part_points[1].T.reshape(-1),
            part_points[2].T.reshape(-1),
        )
        total = total + jnp.sum(kernel_block, axis=1)
        offset = (first_element + first) // EY * EY
        local = (part_links - offset) % M
        ones = (local[:, :, None] == window_iota[None, None, :]).astype(jnp.float32)
        trial_phi = jnp.einsum(
            "eka,eaw->ekw", local_values(part_extract), ones, precision=lax.Precision.HIGHEST
        ).reshape(span * QP, width)
        block = jnp.dot(
            kernel_block,
            trial_phi,
            precision=lax.Precision.HIGHEST,
            preferred_element_type=jnp.float32,
        )
        current = lax.dynamic_slice_in_dim(potential_wide, offset, width, 1)
        potential_wide = lax.dynamic_update_slice_in_dim(potential_wide, current + block, offset, 1)
        return (potential_wide, total)

    return lax.fori_loop(0, count // span, step, state)


def shards(conn, extract, points):
    count = conn.shape[0]
    rows = count * QP
    links_flat = conn.T
    extract_flat = extract.reshape(QP * QP, count)
    points_flat = points.reshape(3 * QP, count)
    own_x = points[0].T.reshape(-1)
    own_y = points[1].T.reshape(-1)
    own_w = points[2].T.reshape(-1)
    own_values = local_values(extract)
    test_phi = basis_rows(own_values, conn)
    width = window_width()
    start_state = (jnp.zeros((rows, M + width), jnp.float32), jnp.zeros((rows,), jnp.float32))
    grid_size = lax.axis_size("grid")
    blk_size = lax.axis_size("blk")
    grid_at = lax.axis_index("grid")
    blk_at = lax.axis_index("blk")
    tile_rows = M // (TB * grid_size)
    tile_cols = M // (TB * blk_size)
    band = tile_cols * TB
    potential_wide, total = add_potential(
        start_state,
        (
            lax.all_gather(points_flat, ("blk", "grid"), axis=1, tiled=True),
            lax.all_gather(extract_flat, ("blk", "grid"), axis=1, tiled=True),
            lax.all_gather(links_flat, ("blk", "grid"), axis=1, tiled=True),
        ),
        jnp.int32(0),
        own_x,
        own_y,
    )
    potential = fold_window(potential_wide)
    share = own_w[:, None] * ((mass_shift + total)[:, None] * test_phi - potential)
    own_contrib = jnp.einsum(
        "eka,ekm->eam", own_values, share.reshape(count, QP, M), precision=lax.Precision.HIGHEST
    )
    split_cols = (
        own_contrib.reshape(rows, tile_cols, blk_size, TB)
        .transpose(2, 0, 1, 3)
        .reshape(blk_size, rows, band)
    )
    targets = tile_target(conn.reshape(-1), grid_size, tile_rows)
    placed = (
        jnp.zeros((blk_size, grid_size * tile_rows * TB, band), jnp.float32)
        .at[:, targets]
        .add(split_cols)
    )
    term = placed.reshape(blk_size * grid_size, -1)
    stiff = lax.psum_scatter(term, ("blk", "grid"), scatter_dimension=0, tiled=True).reshape(
        tile_rows, TB, tile_cols, TB
    )
    column_tiles = stiff[:, :, 0, :]
    mine = spread(column_tiles, "blk", 0)
    panel_tiles = lax.all_gather(mine, "grid", axis=0, tiled=True)
    panel = panel_tiles.reshape(grid_size, tile_rows, TB, TB).transpose(1, 0, 2, 3).reshape(M, TB)
    head = panel[:TB]
    lower = jnp.linalg.cholesky(0.5 * (head + head.T))
    rest = lax.linalg.triangular_solve(
        lower, panel[TB:], left_side=False, lower=True, transpose_a=True
    )
    factor_cols = jnp.concatenate([lower, rest], axis=0)
    row_part = lax.dynamic_index_in_dim(
        factor_cols.reshape(tile_rows, grid_size, TB, TB), grid_at, 1, keepdims=False
    )
    col_part = lax.dynamic_index_in_dim(
        factor_cols.reshape(tile_cols, blk_size, TB, TB), blk_at, 1, keepdims=False
    )
    update = jnp.einsum("xuw,yvw->xuyv", row_part, col_part, precision=lax.Precision.HIGHEST)
    tile_row = (jnp.arange(tile_rows, dtype=jnp.int32) * grid_size + grid_at)[:, None, None, None]
    tile_col = (jnp.arange(tile_cols, dtype=jnp.int32) * blk_size + blk_at)[None, None, :, None]
    whole_row = tile_row * TB + jnp.arange(TB, dtype=jnp.int32)[None, :, None, None]
    whole_col = tile_col * TB + jnp.arange(TB, dtype=jnp.int32)[None, None, None, :]
    trailing = stiff - update
    result = jnp.where(
        tile_col == 0, row_part[:, :, None, :], jnp.where(tile_row == 0, 0.0, trailing)
    )
    return jnp.where(whole_row >= whole_col, result, 0.0)


def solution(mesh):
    in_specs = (
        P(("blk", "grid"), None),
        P(None, None, ("blk", "grid")),
        P(None, None, ("blk", "grid")),
    )
    out_specs = P(None, "grid", None, "blk")
    return jax.shard_map(shards, mesh=mesh, in_specs=in_specs, out_specs=out_specs, check_vma=False)
```

profile of v0, /device:TPU:1, one launch (start us, length us, event | category | flops | bytes accessed | tf_op | source)
XLA Modules:
  0.0 1185.3 jit_solution(11756267952525601225)
XLA Ops:
  13.7 182.9 %all_gather.13 = f32[81,2048]{0,1:T(8,128)S(1)} all-gather(f32[81,16]{0,1:T(8,128)S(1)} %copy.82), channel_id=1, replica_groups=mesh['blk'=8,'grid'=16] {'blk','grid'}, dimensions={1}, use_global_device_ids=true | all-gather | bytes 668736 | tf_op jit(solution)/shard_map/all_gather | solution.py:146
  197.9 183.5 %all_gather.12 = f32[27,2048]{0,1:T(8,128)} all-gather(f32[27,16]{0,1:T(8,128)S(1)} %reshape.418), channel_id=1, replica_groups=mesh['blk'=8,'grid'=16] {'blk','grid'}, dimensions={1}, use_global_device_ids=true | all-gather | bytes 222912 | tf_op jit(solution)/shard_map/all_gather | solution.py:145
  381.4 184.8 %all_gather.14 = s32[9,2048]{0,1:T(8,128)} all-gather(s32[9,16]{0,1:T(8,128)S(1)} %bitcast.107), channel_id=1, replica_groups=mesh['blk'=8,'grid'=16] {'blk','grid'}, dimensions={1}, use_global_device_ids=true | all-gather | bytes 74304 | tf_op jit(solution)/shard_map/all_gather | solution.py:147
  568.2 172.8 %while.20 = (s32[]{:T(128)}, f32[144,2304]{1,0:T(8,128)}, f32[144]{0:T(256)S(1)}, f32[27,2048]{0,1:T(8,128)}, f32[16,9]{1,0:T(8,128)}, /*index=5*/f32[16,9]{1,0:...) while((s32[]{:T(128)}, f32[144,2304]{1,0:T(8,128)}, ...), condition=%wide.wide.region_2.3_spmd.clone.clone, body=%wide.wide.region_0.2_spmd.sunk.clone.clone.sunk | while | flops 548399360 | bytes 5783860 | solution.py:119
  570.6 1.5 fusion.61
  574.0 2.4 convolution_add_fusion.3
  576.4 1.7 dynamic_update_slice.15
  581.4 1.5 fusion.61
  584.8 2.4 convolution_add_fusion.3
  587.2 1.7 dynamic_update_slice.15
  592.3 1.5 fusion.61
  595.7 2.4 convolution_add_fusion.3
  598.1 1.7 dynamic_update_slice.15
  603.1 1.5 fusion.61
  606.5 2.4 convolution_add_fusion.3
  608.9 1.7 dynamic_update_slice.15
  613.9 1.5 fusion.61
  617.3 2.4 convolution_add_fusion.3
  619.7 1.7 dynamic_update_slice.15
  624.6 1.5 fusion.61
  628.0 2.4 convolution_add_fusion.3
  630.4 1.7 dynamic_update_slice.15
  638.8 2.4 convolution_add_fusion.3
  641.2 1.7 dynamic_update_slice.15
  646.2 1.5 fusion.61
  649.6 2.4 convolution_add_fusion.3
  652.0 1.7 dynamic_update_slice.15
  657.1 1.5 fusion.61
  660.5 2.4 convolution_add_fusion.3
  662.9 1.7 dynamic_update_slice.15
  667.9 1.5 fusion.61
  671.3 2.4 convolution_add_fusion.3
  673.7 1.7 dynamic_update_slice.15
  678.7 1.5 fusion.61
  682.1 2.4 convolution_add_fusion.3
  684.5 1.7 dynamic_update_slice.15
  689.5 1.5 fusion.61
  692.9 2.4 convolution_add_fusion.3
  695.3 1.7 dynamic_update_slice.15
  700.3 1.5 fusion.61
  703.7 2.4 convolution_add_fusion.3
  706.1 1.7 dynamic_update_slice.15
  711.1 1.5 fusion.61
  714.5 2.4 convolution_add_fusion.3
  716.9 1.7 dynamic_update_slice.15
  721.9 1.5 fusion.61
  725.3 2.4 convolution_add_fusion.3
  727.7 1.7 dynamic_update_slice.15
  732.7 1.5 fusion.61
  736.1 2.4 convolution_add_fusion.3
  738.5 1.7 dynamic_update_slice.15
  745.1 10.7 scatter_custom_fusion.1
  757.6 1.5 subtract_multiply_fusion
  759.3 3.3 fusion.33
  762.6 1.6 reshape.384
  764.3 6.0 broadcast_in_dim.83
  770.3 16.2 %scatter_fusion = f32[8,2048,256]{2,0,1:T(8,128)} fusion(f32[8,2048,256]{2,0,1:T(8,128)} %broadcast_in_dim.83, s32[144]{0:T(256)S(1)} %bitcast.113, f32[144,8,256]{2,1,0:T(8,128)S(1)} %bitcast.99), kind=kCustom, calls=%fused_computation | custom fusion | flops 294912 | bytes 3539520 | tf_op jit(solution)/shard_map/scatter-add | solution.py:167
  786.4 15.8 %copy.93 = f32[8,2048,256]{2,1,0:T(8,128)} copy(f32[8,2048,256]{2,0,1:T(8,128)} %scatter_fusion) | data formatting | bytes 33554432 | tf_op jit(solution)/shard_map/scatter-add | solution.py:167
  802.3 18.2 %reshape.386 = f32[128,32768]{1,0:T(8,128)} reshape(f32[8,2048,256]{2,1,0:T(8,128)} %copy.93) | data formatting | bytes 33554432 | tf_op jit(solution)/shard_map/reshape | solution.py:169
  820.6 210.2 %all-reduce.7.cloned.1.call-done = f32[128,32768]{1,0:T(8,128)} async-done(((f32[128,32768]{1,0:T(8,128)}), f32[128,32768]{1,0:T(8,128)}) %all-reduce.7.cloned.1.call-update) | async-done | bytes 16777232
  1033.1 66.6 %all-reduce.5.cloned.1.call-done = f32[1,128,128]{2,1,0:T(8,128)} async-done(((f32[1,128,128]{2,1,0:T(8,128)}), f32[1,128,128]{2,1,0:T(8,128)}) %all-reduce.5.cloned.1.call-update) | async-done | bytes 65552 | tf_op jit(solution)/shard_map/psum | solution.py:18
  1099.9 52.0 %all-gather.2.cloned.1.call-done = f32[16,128,128]{2,1,0:T(8,128)} async-done(((f32[1,128,128]{2,1,0:T(8,128)}), f32[16,128,128]{2,1,0:T(8,128)}) %all-gather.2.cloned.1.call-update) | async-done | bytes 1048592 | tf_op jit(solution)/shard_map/all_gather | solution.py:175
  1153.8 11.7 cholesky.18
  1166.9 9.8 custom-call.6
  (281 shorter events, 107.1 us)
Async XLA Ops:
  6.5 1024.2 %all-reduce.7.cloned.1.call-start = ((), (), s32[]{:S(2)}) async-start(), calls=%async_computation.2 | async-start | bytes 33554432
  12.4 185.4 %copy-start.4 = (f32[1,9,16]{1,2,0:T(8,128)}, f32[1,9,16]{1,2,0:T(8,128)S(1)}, u32[]{:S(2)}) copy-start(f32[1,9,16]{1,2,0:T(8,128)S(1)} %copy.103) | copy-start | bytes 1732
  12.6 185.2 %copy-start.5 = (f32[1,9,16]{1,2,0:T(8,128)}, f32[1,9,16]{1,2,0:T(8,128)S(1)}, u32[]{:S(2)}) copy-start(f32[1,9,16]{1,2,0:T(8,128)S(1)} %copy.102) | copy-start | bytes 1732
  196.6 184.8 %copy-start.3 = (s32[16,9]{1,0:T(8,128)S(1)}, s32[16,9]{1,0:T(8,128)}, u32[]{:S(2)}) copy-start(s32[16,9]{1,0:T(8,128)} %param.7) | copy-start | bytes 1732
  197.8 368.3 %copy-start.1 = (f32[9,9,1]{1,0,2:T(8,128)S(1)}, f32[9,9,1]{1,0,2:T(8,128)}, u32[]{:S(2)}) copy-start(f32[9,9,1]{1,0,2:T(8,128)} %constant.314) | copy-start | bytes 976
  197.8 368.3 %copy-start.2 = (f32[9,9,16]{2,1,0:T(8,128)S(1)}, f32[9,9,16]{2,1,0:T(8,128)}, u32[]{:S(2)}) copy-start(f32[9,9,16]{2,1,0:T(8,128)} %param.8) | copy-start | bytes 15556
  568.2 174.9 %copy-start.9 = (s32[2]{0:T(128)S(1)}, s32[2]{0:T(128)}, u32[]{:S(2)}) copy-start(s32[2]{0:T(128)} %constant.303) | copy-start | bytes 28
  568.2 175.1 %copy-start.8 = (s32[2]{0:T(128)S(1)}, s32[2]{0:T(128)}, u32[]{:S(2)}) copy-start(s32[2]{0:T(128)} %constant.306) | copy-start | bytes 28
  755.8 1.2 copy-start.6
  755.9 1.8 copy-start
  762.6 1.6 copy-start.7
  820.5 279.2 %all-reduce.5.cloned.1.call-start = ((), (), s32[]{:S(2)}) async-start(), calls=%async_computation | async-start | bytes 131072 | tf_op jit(solution)/shard_map/psum | solution.py:18
  1032.8 119.1 %all-gather.2.cloned.1.call-start = ((), (), s32[]{:S(2)}) async-start(), calls=%async_computation.1 | async-start | bytes 1114112 | tf_op jit(solution)/shard_map/all_gather | solution.py:175
  1153.7 23.0 %slice-start = ((f32[16,128,128]{2,1,0:T(8,128)}), f32[15,128,128]{2,1,0:T(8,128)S(1)}, s32[]{:S(2)}) async-start(f32[16,128,128]{2,1,0:T(8,128)} %all-gather.2.cloned.1.call-done), calls=%async_computation.3 | async-start | bytes 1966080 | tf_op jit(solution)/shard_map/slice | solution.py:180
Sparse Core Ops, SparseCore 0:
  820.6 210.1 all-reduce.6
  1033.4 66.3 all-reduce.4
  1102.2 49.6 all-gather.1
where the time goes:
time: 1190 us
  blocking collectives  551 us (46%)
  waiting for transfers between devices  329 us (28%)
  local copies, waits for them, and re-layouts  120 us (10%)
  other arithmetic  99.5 us (8%)
  matrix products  70.7 us (6%)
  between operations  13.4 us (1%)
    unnamed x4, waiting for transfers between devices  210 us
    all_gather x1, blocking collectives, shards(): lax.all_gather(links_flat, ('blk', 'grid'), axis=1, tiled=True)  185 us
    all_gather x1, blocking collectives, shards(): lax.all_gather(points_flat, ('blk', 'grid'), axis=1, tiled=True)  183 us
    all_gather x1, blocking collectives, shards(): lax.all_gather(extract_flat, ('blk', 'grid'), axis=1, tiled=True)  183 us
    psum x1, waiting for transfers between devices, spread(): return lax.psum(jnp.where(mine, array, jnp.zeros_like(array)), axis)  66.6 us
    all_gather x1, waiting for transfers between devices, shards(): panel_tiles = lax.all_gather(mine, 'grid', axis=0, tiled=True)  52 us
    dot_general x16, matrix products, step(): jnp.dot(kernel_block, trial_phi, precision=lax.Precision.HIGHEST, preferr...  38.3 us
    dynamic_update_slice x16, local copies, waits for them, and re-layouts, step(): lax.dynamic_update_slice_in_dim(potential_wide, current + block, offset, 1)  27.4 us
  transfers between devices with their start and end apart: 3, of which 3 were waited for; matrix products, arithmetic and copies ran while one was open for 0% of the time, Pallas kernels for 0%

commit v1 on v0

--- a/solution.py
+++ b/solution.py
@@ -144,7 +144,15 @@
         (
             lax.all_gather(points_flat, ("blk", "grid"), axis=1, tiled=True),
             lax.all_gather(extract_flat, ("blk", "grid"), axis=1, tiled=True),
-            lax.all_gather(links_flat, ("blk", "grid"), axis=1, tiled=True),
+            jnp.concatenate(
+                lax.all_to_all(
+                    jnp.stack([links_flat] * lax.axis_size(("blk", "grid")), axis=0),
+                    ("blk", "grid"),
+                    0,
+                    0,
+                ),
+                axis=1,
+            ),
         ),
         jnp.int32(0),
         own_x,

time: 1190 us -> 1010 us (0.85)
  blocking collectives: 551 us -> 365 us
    all_gather x1 -> x0, blocking collectives: 185 us -> none  [shards(): lax.all_gather(links_flat, ('blk', 'grid'), axis=1, tiled=True)]
  transfers between devices with their start and end apart: 3 -> 4, of which waited for: 3 -> 3; matrix products, arithmetic and copies ran while one was open for 0% -> 2% of each run, Pallas kernels for 0% -> 0%
where the time goes in v1:
time: 1010 us
  blocking collectives  365 us (36%)
  waiting for transfers between devices  330 us (33%)
  local copies, waits for them, and re-layouts  118 us (12%)
  other arithmetic  98.6 us (10%)
  matrix products  70 us (7%)
  between operations  13.5 us (1%)
  starting transfers between devices  11.8 us (1%)
    unnamed x4, waiting for transfers between devices  211 us
    all_gather x1, blocking collectives, shards(): lax.all_gather(points_flat, ('blk', 'grid'), axis=1, tiled=True)  184 us
    all_gather x1, blocking collectives, shards(): lax.all_gather(extract_flat, ('blk', 'grid'), axis=1, tiled=True)  181 us
    psum x1, waiting for transfers between devices, spread(): return lax.psum(jnp.where(mine, array, jnp.zeros_like(array)), axis)  66.6 us
    all_gather x1, waiting for transfers between devices, shards(): panel_tiles = lax.all_gather(mine, 'grid', axis=0, tiled=True)  52 us
    dot_general x16, matrix products, step(): jnp.dot(kernel_block, trial_phi, precision=lax.Precision.HIGHEST, preferr...  38.3 us
    dynamic_update_slice x16, local copies, waits for them, and re-layouts, step(): lax.dynamic_update_slice_in_dim(potential_wide, current + block, offset, 1)  27.4 us
    dot_general x16, matrix products, step(): jnp.einsum('eka,eaw->ekw', local_values(part_extract), ones, precision=la...  23.8 us
  transfers between devices with their start and end apart: 4, of which 3 were waited for; matrix products, arithmetic and copies ran while one was open for 2% of the time, Pallas kernels for 0%

profile of v1, /device:TPU:1, one launch (start us, length us, event | category | flops | bytes accessed | tf_op | source)
XLA Modules:
  0.0 1008.1 jit_solution(8382467382901378249)
XLA Ops:
  8.8 11.5 %all-to-all-start = ((s32[128,1,144]{2,1,0:T(1,128)}), s32[128,1,144]{2,1,0:T(1,128)S(1)}, u32[]{:S(2)}, u32[]{:S(2)}) async-start(s32[128,1,144]{2,1,0:T(1,128)} %reshape.431), calls=%async_computation | async-start | bytes 262144 | tf_op jit(solution)/shard_map/all_to_all | solution.py:148
  21.2 181.1 %all_gather.10 = f32[81,2048]{0,1:T(8,128)S(1)} all-gather(f32[81,16]{0,1:T(8,128)S(1)} %copy.82), channel_id=1, replica_groups=mesh['blk'=8,'grid'=16] {'blk','grid'}, dimensions={1}, use_global_device_ids=true | all-gather | bytes 668736 | tf_op jit(solution)/shard_map/all_gather | solution.py:146
  205.5 10.5 %scatter_custom_fusion.1 = f32[294912]{0:T(1024)S(1)} fusion(s32[1296]{0:T(1024)S(1)} %reshape.417, f32[1296]{0:T(1024)S(1)} %reshape.419, f32[]{:T(128)} %constant.282.clone.1), kind=kCustom, calls=%fused_computation.32 | custom fusion | flops 1296 | bytes 1179652
  217.5 183.5 %all_gather.9 = f32[27,2048]{0,1:T(8,128)} all-gather(f32[27,16]{0,1:T(8,128)S(1)} %reshape.428), channel_id=1, replica_groups=mesh['blk'=8,'grid'=16] {'blk','grid'}, dimensions={1}, use_global_device_ids=true | all-gather | bytes 222912 | tf_op jit(solution)/shard_map/all_gather | solution.py:145
  402.5 1.6 reshape.432
  405.3 172.8 %while.20 = (s32[]{:T(128)}, f32[144,2304]{1,0:T(8,128)}, f32[144]{0:T(256)S(1)}, f32[27,2048]{0,1:T(8,128)}, f32[16,9]{1,0:T(8,128)}, /*index=5*/f32[16,9]{1,0:...) while((s32[]{:T(128)}, f32[144,2304]{1,0:T(8,128)}, ...), condition=%wide.wide.region_2.3_spmd.clone.clone, body=%wide.wide.region_0.2_spmd.sunk.clone.clone.sunk | while | flops 548399360 | bytes 5783860 | solution.py:119
  407.7 1.5 fusion.61
  411.1 2.4 convolution_add_fusion.3
  413.5 1.7 dynamic_update_slice.15
  418.5 1.5 fusion.61
  421.9 2.4 convolution_add_fusion.3
  424.3 1.7 dynamic_update_slice.15
  429.3 1.5 fusion.61
  432.7 2.4 convolution_add_fusion.3
  435.1 1.7 dynamic_update_slice.15
  440.1 1.5 fusion.61
  443.5 2.4 convolution_add_fusion.3
  445.9 1.7 dynamic_update_slice.15
  450.9 1.5 fusion.61
  454.3 2.4 convolution_add_fusion.3
  456.7 1.7 dynamic_update_slice.15
  461.7 1.5 fusion.61
  465.1 2.4 convolution_add_fusion.3
  467.5 1.7 dynamic_update_slice.15
  475.9 2.4 convolution_add_fusion.3
  478.3 1.7 dynamic_update_slice.15
  483.3 1.5 fusion.61
  486.7 2.4 convolution_add_fusion.3
  489.1 1.7 dynamic_update_slice.15
  494.1 1.5 fusion.61
  497.5 2.4 convolution_add_fusion.3
  499.9 1.7 dynamic_update_slice.15
  504.9 1.5 fusion.61
  508.3 2.4 convolution_add_fusion.3
  510.7 1.7 dynamic_update_slice.15
  519.2 2.4 convolution_add_fusion.3
  521.6 1.7 dynamic_update_slice.15
  526.6 1.5 fusion.61
  530.0 2.4 convolution_add_fusion.3
  532.4 1.7 dynamic_update_slice.15
  537.4 1.5 fusion.61
  540.8 2.4 convolution_add_fusion.3
  543.2 1.7 dynamic_update_slice.15
  548.2 1.5 fusion.61
  551.6 2.4 convolution_add_fusion.3
  554.0 1.7 dynamic_update_slice.15
  559.0 1.5 fusion.61
  562.4 2.4 convolution_add_fusion.3
  564.8 1.7 dynamic_update_slice.15
  569.8 1.5 fusion.61
  573.2 2.4 convolution_add_fusion.3
  575.6 1.7 dynamic_update_slice.15
  579.0 1.9 subtract_multiply_fusion
  581.1 3.3 fusion.33
  584.4 1.6 reshape.394
  586.0 6.0 broadcast_in_dim.83
  592.0 16.2 %scatter_fusion = f32[8,2048,256]{2,0,1:T(8,128)} fusion(f32[8,2048,256]{2,0,1:T(8,128)} %broadcast_in_dim.83, s32[144]{0:T(256)S(1)} %bitcast.119, f32[144,8,256]{2,1,0:T(8,128)S(1)} %bitcast.105), kind=kCustom, calls=%fused_computation | custom fusion | flops 294912 | bytes 3539520 | tf_op jit(solution)/shard_map/scatter-add | solution.py:175
  608.2 15.8 %copy.93 = f32[8,2048,256]{2,1,0:T(8,128)} copy(f32[8,2048,256]{2,0,1:T(8,128)} %scatter_fusion) | data formatting | bytes 33554432 | tf_op jit(solution)/shard_map/scatter-add | solution.py:175
  624.0 18.2 %reshape.396 = f32[128,32768]{1,0:T(8,128)} reshape(f32[8,2048,256]{2,1,0:T(8,128)} %copy.93) | data formatting | bytes 33554432 | tf_op jit(solution)/shard_map/reshape | solution.py:177
  642.3 211.3 %all-reduce.7.cloned.1.call-done = f32[128,32768]{1,0:T(8,128)} async-done(((f32[128,32768]{1,0:T(8,128)}), f32[128,32768]{1,0:T(8,128)}) %all-reduce.7.cloned.1.call-update) | async-done | bytes 16777232
  855.9 66.6 %all-reduce.5.cloned.1.call-done = f32[1,128,128]{2,1,0:T(8,128)} async-done(((f32[1,128,128]{2,1,0:T(8,128)}), f32[1,128,128]{2,1,0:T(8,128)}) %all-reduce.5.cloned.1.call-update) | async-done | bytes 65552 | tf_op jit(solution)/shard_map/psum | solution.py:18
  922.7 52.0 %all-gather.2.cloned.1.call-done = f32[16,128,128]{2,1,0:T(8,128)} async-done(((f32[1,128,128]{2,1,0:T(8,128)}), f32[16,128,128]{2,1,0:T(8,128)}) %all-gather.2.cloned.1.call-update) | async-done | bytes 1048592 | tf_op jit(solution)/shard_map/all_gather | solution.py:183
  976.6 11.7 %cholesky.18 = f32[128,128]{1,0:T(8,128)S(1)} custom-call(f32[128,128]{1,0:T(8,128)S(1)} %fusion.23), custom_call_target="Cholesky" | custom-call | tf_op jit(solution)/shard_map/jit(cholesky)/cholesky | solution.py:186
  989.7 9.8 custom-call.6
  (282 shorter events, 103.5 us)
Async XLA Ops:
  6.5 14.0 %copy-start.2 = (s32[16,9]{1,0:T(8,128)S(1)}, s32[16,9]{1,0:T(8,128)}, u32[]{:S(2)}) copy-start(s32[16,9]{1,0:T(8,128)} %param.7) | copy-start | bytes 1732
  6.5 13.8 %copy-start.3 = (f32[3,9,16]{2,0,1:T(4,128)S(1)}, f32[3,9,16]{2,0,1:T(4,128)}, u32[]{:S(2)}) copy-start(f32[3,9,16]{2,0,1:T(4,128)} %param.9) | copy-start | bytes 5188
  6.5 14.5 %copy-start.1 = (f32[9,9,16]{2,1,0:T(8,128)S(1)}, f32[9,9,16]{2,1,0:T(8,128)}, u32[]{:S(2)}) copy-start(f32[9,9,16]{2,1,0:T(8,128)} %param.8) | copy-start | bytes 15556
  8.8 392.2 %all-to-all-start = ((s32[128,1,144]{2,1,0:T(1,128)}), s32[128,1,144]{2,1,0:T(1,128)S(1)}, u32[]{:S(2)}, u32[]{:S(2)}) async-start(s32[128,1,144]{2,1,0:T(1,128)} %reshape.431), calls=%async_computation | async-start | bytes 262144 | tf_op jit(solution)/shard_map/all_to_all | solution.py:148
  20.3 833.3 %all-reduce.7.cloned.1.call-start = ((), (), s32[]{:S(2)}) async-start(), calls=%async_computation.3 | async-start | bytes 33554432
  20.8 182.7 %copy-start.4 = (f32[1,9,16]{1,2,0:T(8,128)}, f32[1,9,16]{1,2,0:T(8,128)S(1)}, u32[]{:S(2)}) copy-start(f32[1,9,16]{1,2,0:T(8,128)S(1)} %copy.103) | copy-start | bytes 1732
  21.0 182.5 %copy-start.5 = (f32[1,9,16]{1,2,0:T(8,128)}, f32[1,9,16]{1,2,0:T(8,128)S(1)}, u32[]{:S(2)}) copy-start(f32[1,9,16]{1,2,0:T(8,128)S(1)} %copy.102) | copy-start | bytes 1732
  21.2 182.9 %copy-start.7 = (s32[2]{0:T(128)S(1)}, s32[2]{0:T(128)}, u32[]{:S(2)}) copy-start(s32[2]{0:T(128)} %constant.303) | copy-start | bytes 28
  202.3 2.0 copy-start.6
  202.3 2.7 copy-start
  642.2 280.3 %all-reduce.5.cloned.1.call-start = ((), (), s32[]{:S(2)}) async-start(), calls=%async_computation.1 | async-start | bytes 131072 | tf_op jit(solution)/shard_map/psum | solution.py:18
  855.6 119.1 %all-gather.2.cloned.1.call-start = ((), (), s32[]{:S(2)}) async-start(), calls=%async_computation.2 | async-start | bytes 1114112 | tf_op jit(solution)/shard_map/all_gather | solution.py:183
  976.5 23.0 %slice-start = ((f32[16,128,128]{2,1,0:T(8,128)}), f32[15,128,128]{2,1,0:T(8,128)S(1)}, s32[]{:S(2)}) async-start(f32[16,128,128]{2,1,0:T(8,128)} %all-gather.2.cloned.1.call-done), calls=%async_computation.4 | async-start | bytes 1966080 | tf_op jit(solution)/shard_map/slice | solution.py:188
Sparse Core Ops, SparseCore 0:
  642.4 211.1 all-reduce.6
  856.2 66.3 all-reduce.4
  925.0 49.6 all-gather.1
